TPU v7x, 128 devices: a whole 4x4x4 slice. The times are simulated.
128 devices in a mesh: dp: 8 (over z, core), mp: 16 (over y, x).
Axes of the slice: x: 4, y: 4, z: 4, core: 2. Of those that a mesh axis runs over, the one named last changes fastest.
Arguments:
- acts: bfloat16 [1024, 8192], P('dp', 'mp'), may hold values from -6 to 6
- w_up: bfloat16 [8192, 14336], P(None, 'mp'), may hold values from -0.0625 to 0.0625
- out_grad: bfloat16 [1024, 14336], P('dp', 'mp'), may hold values from -6 to 6
- rotation: float32 [8192, 8192], P('mp', 'dp'), may hold values from -6 to 6
Outputs:
- half_rotation: float32 [8192, 8192], P('mp', 'dp')
- next_rotation: float32 [8192, 8192], P('mp', 'dp')
All inputs are finite; a program needn't handle non-finite values.
Results may differ from a plain program's by a relative error of at most 0.017.
Values may be sent and summed in bfloat16 or wider, within the bound.
A program may use at most 128 MiB of HBM per device.

v0:
```python
import functools
import math
import jax
import jax.numpy as jnp
from jax import lax
from jax.sharding import Mesh
from jax.sharding import PartitionSpec as P

D = 8192
ITERS = 2
DP = ("dp_0", "dp_1")
MP = ("mp_0", "mp_1")
DP_MP = ("dp_0", "dp_1", "mp_0", "mp_1")
step_gain = 0.5
epsilon = 1e-06


def by_axis(value, axes):
    return functools.reduce(lax.psum, axes, value)


def in_one_piece(arrays, axis, dim, along):
    both = jnp.concatenate(arrays, axis=along)
    filled, at, gathered = (lax.all_gather(both, axis, axis=dim, tiled=True), 0, [])
    for a in arrays:
        gathered.append(lax.slice_in_dim(filled, at, at + a.shape[along], axis=along))
        at += a.shape[along]
    return tuple(gathered)


def settle(term):
    return lax.optimization_barrier(term.astype(jnp.bfloat16)).astype(jnp.float32)


def contract_cols(left, right):
    return lax.dot_general(
        left, right, (((1,), (1,)), ((), ())), preferred_element_type=jnp.float32
    )


def local(acts, w_up, out_grad, rotation):
    inv_root = D ** (-0.5)
    rot_half = rotation.astype(jnp.bfloat16)
    rot_rows = lax.all_gather(rot_half, DP, axis=1, tiled=True)
    mixed = lax.psum(
        (jnp.dot(acts, rot_rows, preferred_element_type=jnp.float32) * inv_root).astype(
            jnp.bfloat16
        ),
        MP,
    )
    hidden = jnp.dot(mixed, w_up, preferred_element_type=jnp.float32)
    sigmoid_hidden = jax.nn.sigmoid(hidden)
    grad_hidden = (
        out_grad.astype(jnp.float32) * sigmoid_hidden * (1.0 + hidden * (1.0 - sigmoid_hidden))
    ).astype(jnp.bfloat16)
    grad_mixed = lax.psum(contract_cols(grad_hidden, w_up).astype(jnp.bfloat16), MP)
    factor = contract_cols(grad_mixed, rot_rows).astype(jnp.bfloat16)
    act_norm, factor_norm = (
        by_axis(jnp.sum(jnp.square(acts.astype(jnp.float32))), DP_MP),
        by_axis(jnp.sum(jnp.square(factor.astype(jnp.float32))), DP_MP),
    )
    token_count = acts.shape[0] * lax.axis_size(DP)
    spread = (token_count ** (-0.5) + D ** (-0.5)) ** 2
    step_size = (
        step_gain
        * math.sqrt(D)
        / (jnp.sqrt((act_norm + epsilon) * (factor_norm + epsilon)) * spread)
    )
    every_acts, every_factor = in_one_piece((acts, factor), DP, 0, 1)
    groups = lax.axis_size(DP)
    block_rows = acts.shape[0]
    acts_blocks = every_acts.reshape(groups, block_rows, -1)
    factor_blocks = every_factor.reshape(groups, block_rows, -1)
    current = rotation
    first_iterate = rotation
    for iteration in range(ITERS):
        point = (rotation + current).astype(jnp.bfloat16)
        left_sum, right_sum = (
            lax.psum(
                (
                    jnp.dot(every_factor, point, preferred_element_type=jnp.float32) * inv_root
                ).astype(jnp.bfloat16),
                MP,
            ).astype(jnp.float32),
            lax.psum(
                (jnp.dot(every_acts, point, preferred_element_type=jnp.float32) * inv_root).astype(
                    jnp.bfloat16
                ),
                MP,
            ).astype(jnp.float32),
        )
        left = left_sum.astype(jnp.bfloat16).reshape(groups, block_rows, -1)
        right = right_sum.astype(jnp.bfloat16).reshape(groups, block_rows, -1)
        terms = jnp.einsum(
            "ntr,ntc->nrc", acts_blocks, left, preferred_element_type=jnp.float32
        ) - jnp.einsum("ntr,ntc->nrc", factor_blocks, right, preferred_element_type=jnp.float32)
        update = jnp.sum(settle(terms), axis=0)
        current = rotation - step_size * update
        if iteration == 0:
            first_iterate = current
    return (first_iterate, current)


def solution(mesh):
    finer = Mesh(mesh.devices.reshape(4, 2, 4, 4), ("dp_0", "dp_1", "mp_0", "mp_1"))
    placed = (P(DP, MP), P(None, MP), P(DP, MP), P(MP, DP))
    return jax.shard_map(
        local, mesh=finer, in_specs=placed, out_specs=(P(MP, DP), P(MP, DP)), check_vma=False
    )
```

profile of v0, /device:TPU:1, one launch (start us, length us, event | category | flops | bytes accessed | tf_op | source)
XLA Modules:
  0.0 586.6 jit_solution(2937792211861183039)
XLA Ops:
  7.2 2.8 convert_element_type.64
  10.0 53.8 %all-gather.3.cloned.1.call-done = bf16[512,8192]{1,0:T(8,128)(2,1)} async-done(((bf16[512,1024]{1,0:T(8,128)(2,1)}), bf16[512,8192]{1,0:T(8,128)(2,1)}) %all-gather.3.cloned.1.call-update) | async-done | bytes 8388624 | tf_op jit(solution)/shard_map/all_gather | solution.py:44
  63.8 6.0 %fusion = bf16[128,8192]{1,0:T(8,128)(2,1)} fusion(bf16[128,512]{1,0:T(8,128)(2,1)S(1)} %copy-done.7, bf16[512,8192]{1,0:T(8,128)(2,1)} %all-gather.3.cloned.1.call-done), kind=kOutput, calls=%fused_computation.5 | convolution fusion | flops 1075838976 | bytes 10616832 | tf_op jit(solution)/shard_map/dot_general | solution.py:46
  69.9 88.7 %all-reduce.11.cloned.1.call-done = bf16[128,8192]{1,0:T(8,128)(2,1)} async-done(((bf16[128,8192]{1,0:T(8,128)(2,1)}), bf16[128,8192]{1,0:T(8,128)(2,1)}) %all-reduce.11.cloned.1.call-update) | async-done | bytes 2097168 | tf_op jit(solution)/shard_map/psum | solution.py:45
  158.6 20.2 %convolution_convert_fusion = bf16[128,8192]{1,0:T(8,128)(2,1)} fusion(bf16[8192,896]{1,0:T(8,128)(2,1)} %param.5, bf16[128,896]{1,0:T(8,128)(2,1)S(1)} %copy-done.8, bf16[128,8192]{1,0:T(8,128)(2,1)} %all-reduce.11.cloned.1.call-done), kind=kOutput, calls=%fused_computation.6 | convolution fusion | flops 3760291840 | bytes 19103744 | tf_op jit(solution)/shard_map/dot_general | solution.py:36
  178.9 89.5 %all-reduce.13.cloned.1.call-done = bf16[128,8192]{1,0:T(8,128)(2,1)} async-done(((bf16[128,8192]{1,0:T(8,128)(2,1)}), bf16[128,8192]{1,0:T(8,128)(2,1)}) %all-reduce.13.cloned.1.call-update) | async-done | bytes 2097168 | tf_op jit(solution)/shard_map/psum | solution.py:56
  268.4 7.7 %multiply_reduce_fusion = (f32[]{:T(128)}, bf16[128,512]{1,0:T(8,128)(2,1)S(1)}) fusion(bf16[128,8192]{1,0:T(8,128)(2,1)} %all-reduce.13.cloned.1.call-done, bf16[512,8192]{1,0:T(8,128)(2,1)} %all-gather.3.cloned.1.call-done), kind=kOutput, calls=%fused_computation.18 | convolution fusion | flops 1074003968 | bytes 10616836 | tf_op jit(solution)/shard_map/dot_general | solution.py:36
  276.9 26.4 %all-gather.5.cloned.1.call-done = bf16[1024,1024]{1,0:T(8,128)(2,1)} async-done(((bf16[128,1024]{1,0:T(8,128)(2,1)}), bf16[1024,1024]{1,0:T(8,128)(2,1)}) %all-gather.5.cloned.1.call-update) | async-done | bytes 2097168 | tf_op jit(solution)/shard_map/all_gather | solution.py:24
  303.3 4.0 multiply_convert_fusion.3
  307.2 2.6 multiply_convert_fusion.2
  310.6 7.9 %all-reduce.2 = (f32[]{:T(128)}, f32[]{:T(128)}) all-reduce(f32[]{:T(128)} %multiply_reduce_fusion.1, f32[]{:T(128)} %get-tuple-element.18), channel_id=1, replica_groups=mesh['dp_0'=4,'dp_1'=2,'mp_0'=4,'mp_1'=4] {'dp_0'}, use_global_device_ids=true, to_apply=%region_1.0 | all-reduce | flops 2 | bytes 16 | tf_op jit(solution)/shard_map/psum | solution.py:19
  318.5 5.1 all-reduce.3
  323.6 9.9 %all-reduce.1 = (f32[]{:T(128)}, f32[]{:T(128)}) all-reduce(f32[]{:T(128)} %get-tuple-element.8, f32[]{:T(128)} %get-tuple-element.9), channel_id=1, replica_groups=mesh['dp_0'=4,'dp_1'=2,'mp_0'=4,'mp_1'=4] {'mp_0'}, use_global_device_ids=true, to_apply=%region_3.0 | all-reduce | flops 2 | bytes 16 | tf_op jit(solution)/shard_map/psum | solution.py:19
  333.5 9.3 %all-reduce = (f32[]{:T(128)}, f32[]{:T(128)}) all-reduce(f32[]{:T(128)} %get-tuple-element.4, f32[]{:T(128)} %get-tuple-element.5), channel_id=1, replica_groups=mesh['dp_0'=4,'dp_1'=2,'mp_0'=4,'mp_1'=4] {'mp_1'}, use_global_device_ids=true, to_apply=%region_4.0 | all-reduce | flops 2 | bytes 16 | tf_op jit(solution)/shard_map/psum | solution.py:19
  344.2 2.6 fusion.7
  346.9 66.5 %all-reduce.17.cloned.1.call-done = (bf16[8,128,1024]{2,1,0:T(8,128)(2,1)}, bf16[8,128,1024]{2,1,0:T(8,128)(2,1)}) async-done(((bf16[8,128,1024]{2,1,0:T(8,128)(2,1)}, bf16[8,128,1024]{2,1,0:T(8,128)(2,1)}), (bf16[8,128,1024]{2,1,0:T(8,128)(2,1)}, bf16[8,128,1024]{2,1,0:T(8,128)(2,1)})) %all-reduce.17.cloned.1.call-update) | async-done | bytes 4194320 | tf_op jit(solution)/shard_map/psum | solution.py:79
  413.4 9.8 %fusion.10 = f32[8,512,1024]{2,1,0:T(8,128)} fusion(bf16[8,128,512]{2,1,0:T(8,128)(2,1)S(1)} %bitcast.23, bf16[8,128,1024]{2,1,0:T(8,128)(2,1)} %get-tuple-element.12), kind=kOutput, calls=%fused_computation.28 | convolution fusion | flops 1073741824 | bytes 19922944 | tf_op jit(solution)/shard_map/ntr,ntc->nrc/dot_general | solution.py:94
  423.2 11.4 %subtract_convert_fusion.1 = bf16[8,512,1024]{2,1,0:T(8,128)(2,1)} fusion(f32[8,512,1024]{2,1,0:T(8,128)} %fusion.10, bf16[8,128,512]{2,1,0:T(8,128)(2,1)S(1)} %bitcast.25, bf16[8,128,1024]{2,1,0:T(8,128)(2,1)S(1)} %copy-done.3), kind=kOutput, calls=%fused_computation.3 | convolution fusion | flops 1082130432 | bytes 28311552 | tf_op jit(solution)/shard_map/ntr,ntc->nrc/dot_general | solution.py:96
  434.6 5.7 convert_reduce_fusion.1
  442.2 2.6 multiply_convert_fusion
  447.4 103.4 %all-reduce.15.cloned.1.call-done = (bf16[8,128,1024]{2,1,0:T(8,128)(2,1)}, bf16[8,128,1024]{2,1,0:T(8,128)(2,1)}) async-done(((bf16[8,128,1024]{2,1,0:T(8,128)(2,1)}, bf16[8,128,1024]{2,1,0:T(8,128)(2,1)}), (bf16[8,128,1024]{2,1,0:T(8,128)(2,1)}, bf16[8,128,1024]{2,1,0:T(8,128)(2,1)})) %all-reduce.15.cloned.1.call-update) | async-done | bytes 4194320 | tf_op jit(solution)/shard_map/psum | solution.py:79
  550.8 9.8 %fusion.11 = f32[8,512,1024]{2,1,0:T(8,128)} fusion(bf16[8,128,512]{2,1,0:T(8,128)(2,1)S(1)} %bitcast.24, bf16[8,128,1024]{2,1,0:T(8,128)(2,1)} %get-tuple-element.10), kind=kOutput, calls=%fused_computation.29 | convolution fusion | flops 1073741824 | bytes 19922944 | tf_op jit(solution)/shard_map/ntr,ntc->nrc/dot_general | solution.py:94
  560.7 11.7 %subtract_convert_fusion = bf16[8,512,1024]{2,1,0:T(8,128)(2,1)} fusion(f32[8,512,1024]{2,1,0:T(8,128)} %fusion.11, bf16[8,128,512]{2,1,0:T(8,128)(2,1)S(1)} %bitcast.26, bf16[8,128,1024]{2,1,0:T(8,128)(2,1)S(1)} %copy-done.4), kind=kOutput, calls=%fused_computation.1 | convolution fusion | flops 1082130432 | bytes 28311552 | tf_op jit(solution)/shard_map/ntr,ntc->nrc/dot_general | solution.py:96
  572.3 5.7 convert_reduce_fusion
  (35 shorter events, 8.0 us)
Async XLA Ops:
  7.2 56.7 %copy-start.7 = (bf16[128,512]{1,0:T(8,128)(2,1)S(1)}, bf16[128,512]{1,0:T(8,128)(2,1)}, u32[]{:S(2)}) copy-start(bf16[128,512]{1,0:T(8,128)(2,1)} %param.4) | copy-start | bytes 393220
  7.2 56.7 %all-gather.3.cloned.1.call-start = ((), (), s32[]{:S(2)}) async-start(), calls=%async_computation | async-start | bytes 9437184 | tf_op jit(solution)/shard_map/all_gather | solution.py:44
  10.0 148.6 %all-reduce.11.cloned.1.call-start = ((), (), s32[]{:S(2)}) async-start(), calls=%async_computation.1 | async-start | bytes 4194304 | tf_op jit(solution)/shard_map/psum | solution.py:45
  69.9 88.8 %copy-start.8 = (bf16[128,896]{1,0:T(8,128)(2,1)S(1)}, bf16[128,896]{1,0:T(8,128)(2,1)}, u32[]{:S(2)}) copy-start(bf16[128,896]{1,0:T(8,128)(2,1)} %param.6) | copy-start | bytes 688132
  69.9 198.5 %all-reduce.13.cloned.1.call-start = ((), (), s32[]{:S(2)}) async-start(), calls=%async_computation.2 | async-start | bytes 4194304 | tf_op jit(solution)/shard_map/psum | solution.py:56
  178.8 124.4 %copy-start = (f32[512,1024]{1,0:T(8,128)S(1)}, f32[512,1024]{1,0:T(8,128)}, u32[]{:S(2)}) copy-start(f32[512,1024]{1,0:T(8,128)} %param.7) | copy-start | bytes 6291460
  178.8 124.4 %all-gather.5.cloned.1.call-start = ((), (), s32[]{:S(2)}) async-start(), calls=%async_computation.3 | async-start | bytes 2359296 | tf_op jit(solution)/shard_map/all_gather | solution.py:24
  276.8 136.5 %all-reduce.17.cloned.1.call-start = ((), (), s32[]{:S(2)}) async-start(), calls=%async_computation.5 | async-start | bytes 8388608 | tf_op jit(solution)/shard_map/psum | solution.py:79
  303.3 4.0 copy-start.5
  309.8 241.0 %all-reduce.15.cloned.1.call-start = ((), (), s32[]{:S(2)}) async-start(), calls=%async_computation.4 | async-start | bytes 8388608 | tf_op jit(solution)/shard_map/psum | solution.py:79
  413.4 9.8 %copy-start.1 = (bf16[1024,512]{1,0:T(8,128)(2,1)S(1)}, bf16[1024,512]{1,0:T(8,128)(2,1)}, u32[]{:S(2)}) copy-start(bf16[1024,512]{1,0:T(8,128)(2,1)} %get-tuple-element.16) | copy-start | bytes 3145732
  413.4 9.8 %copy-start.3 = (bf16[8,128,1024]{2,1,0:T(8,128)(2,1)S(1)}, bf16[8,128,1024]{2,1,0:T(8,128)(2,1)}, u32[]{:S(2)}) copy-start(bf16[8,128,1024]{2,1,0:T(8,128)(2,1)} %get-tuple-element.13) | copy-start | bytes 6291460
  440.3 1.9 copy-start.6
  550.8 9.8 %copy-start.2 = (bf16[1024,512]{1,0:T(8,128)(2,1)S(1)}, bf16[1024,512]{1,0:T(8,128)(2,1)}, u32[]{:S(2)}) copy-start(bf16[1024,512]{1,0:T(8,128)(2,1)} %get-tuple-element.16) | copy-start | bytes 3145732
  550.8 9.8 %copy-start.4 = (bf16[8,128,1024]{2,1,0:T(8,128)(2,1)S(1)}, bf16[8,128,1024]{2,1,0:T(8,128)(2,1)}, u32[]{:S(2)}) copy-start(bf16[8,128,1024]{2,1,0:T(8,128)(2,1)} %get-tuple-element.11) | copy-start | bytes 6291460
Sparse Core Ops, SparseCore 0:
  10.3 53.5 all-gather.2
  70.0 88.5 all-reduce.10
  178.9 89.4 all-reduce.12
  276.9 26.2 all-gather.4
  310.0 103.3 all-reduce.16
  447.5 103.2 all-reduce.14
where the time goes:
time: 587 us
  waiting for transfers between devices  428 us (73%)
  matrix products  88.4 us (15%)
  blocking collectives  32.2 us (5%)
  other arithmetic  19.1 us (3%)
  between operations  15.6 us (3%)
    psum x2, waiting for transfers between devices, local(): lax.psum((jnp.dot(every_factor, point, preferred_element_type=jnp.float32...  170 us
    psum x1, waiting for transfers between devices, local(): lax.psum(contract_cols(grad_hidden, w_up).astype(jnp.bfloat16), MP)  89.5 us
    psum x1, waiting for transfers between devices, local(): lax.psum((jnp.dot(acts, rot_rows, preferred_element_type=jnp.float32) * i...  88.7 us
    all_gather x1, waiting for transfers between devices, local(): rot_rows = lax.all_gather(rot_half, DP, axis=1, tiled=True)  53.8 us
    psum x4, blocking collectives, by_axis(): return functools.reduce(lax.psum, axes, value)  32.2 us
    dot_general x2, matrix products, contract_cols(): lax.dot_general(left, right, (((1,), (1,)), ((), ())), preferred_element_...  27.8 us
    all_gather x1, waiting for transfers between devices, in_one_piece(): lax.all_gather(both, axis, axis=dim, tiled=True)  26.4 us
    dot_general x2, matrix products, local(): jnp.einsum('ntr,ntc->nrc', factor_blocks, right, preferred_element_type=j...  23.1 us
  transfers between devices with their start and end apart: 6, of which 6 were waited for; matrix products, arithmetic and copies ran while one was open for 1% of the time, Pallas kernels for 0%

commit v1 on v0

--- a/solution.py
+++ b/solution.py
@@ -41,7 +41,9 @@
 def local(acts, w_up, out_grad, rotation):
     inv_root = D ** (-0.5)
     rot_half = rotation.astype(jnp.bfloat16)
-    rot_rows = lax.all_gather(rot_half, DP, axis=1, tiled=True)
+    rot_rows = jnp.concatenate(
+        lax.all_to_all(jnp.stack([rot_half] * lax.axis_size(DP)), DP, 0, 0), axis=1
+    )
     mixed = lax.psum(
         (jnp.dot(acts, rot_rows, preferred_element_type=jnp.float32) * inv_root).astype(
             jnp.bfloat16

time: 587 us -> 635 us (1.082)
  blocking collectives: 32.2 us -> 134 us
  waiting for transfers between devices: 428 us -> 375 us
    all_to_all x0 -> x1, blocking collectives: none -> 102 us  [local(): lax.all_to_all(jnp.stack([rot_half] * lax.axis_size(DP)), DP, 0, 0)]
    all_gather x1 -> x0, waiting for transfers between devices: 53.8 us -> none  [local(): rot_rows = lax.all_gather(rot_half, DP, axis=1, tiled=True)]
  transfers between devices with their start and end apart: 6 -> 5, of which waited for: 6 -> 5; matrix products, arithmetic and copies ran while one was open for 1% -> 1% of each run, Pallas kernels for 0% -> 0%
where the time goes in v1:
time: 635 us; the launch traced here: 634 us
  waiting for transfers between devices  375 us (59%)
  blocking collectives  134 us (21%)
  matrix products  84.8 us (13%)
  other arithmetic  18.2 us (3%)
  between operations  15.1 us (2%)
  local copies, waits for them, and re-layouts  7.16 us (1%)
    psum x2, waiting for transfers between devices, local(): lax.psum((jnp.dot(every_factor, point, preferred_element_type=jnp.float32...  170 us
    all_to_all x1, blocking collectives, local(): lax.all_to_all(jnp.stack([rot_half] * lax.axis_size(DP)), DP, 0, 0)  102 us
    psum x1, waiting for transfers between devices, local(): lax.psum(contract_cols(grad_hidden, w_up).astype(jnp.bfloat16), MP)  89.6 us
    psum x1, waiting for transfers between devices, local(): lax.psum((jnp.dot(acts, rot_rows, preferred_element_type=jnp.float32) * i...  88.9 us
    psum x4, blocking collectives, by_axis(): return functools.reduce(lax.psum, axes, value)  32.2 us
    all_gather x1, waiting for transfers between devices, in_one_piece(): lax.all_gather(both, axis, axis=dim, tiled=True)  26.4 us
    dot_general x2, matrix products, contract_cols(): lax.dot_general(left, right, (((1,), (1,)), ((), ())), preferred_element_...  26.1 us
    dot_general x2, matrix products, local(): jnp.einsum('ntr,ntc->nrc', factor_blocks, right, preferred_element_type=j...  23.1 us
  transfers between devices with their start and end apart: 5, of which 5 were waited for; matrix products, arithmetic and copies ran while one was open for 1% of the time, Pallas kernels for 0%

profile of v1, /device:TPU:1, one launch (start us, length us, event | category | flops | bytes accessed | tf_op | source)
XLA Modules:
  0.0 634.3 jit_solution(17285620343381976318)
XLA Ops:
  10.3 101.6 %all_to_all.5 = bf16[8,512,1024]{1,2,0:T(8,128)(2,1)S(1)} all-to-all(bf16[8,512,1024]{1,2,0:T(8,128)(2,1)S(1)} %stack.2), channel_id=1, replica_groups=mesh['dp_0'=4,'dp_1'=2,'mp_0'=4,'mp_1'=4] {'dp_0','dp_1'}, dimensions={0} | all-to-all | bytes 16777216 | tf_op jit(solution)/shard_map/all_to_all | solution.py:45
  111.9 3.2 copy-done
  115.1 4.2 fusion
  119.3 88.9 %all-reduce.11.cloned.1.call-done = bf16[128,8192]{1,0:T(8,128)(2,1)} async-done(((bf16[128,8192]{1,0:T(8,128)(2,1)}), bf16[128,8192]{1,0:T(8,128)(2,1)}) %all-reduce.11.cloned.1.call-update) | async-done | bytes 2097168 | tf_op jit(solution)/shard_map/psum | solution.py:47
  208.3 20.2 %convolution_convert_fusion = bf16[128,8192]{1,0:T(8,128)(2,1)} fusion(bf16[8192,896]{1,0:T(8,128)(2,1)} %param.5, bf16[128,896]{1,0:T(8,128)(2,1)S(1)} %copy-done.9, bf16[128,8192]{1,0:T(8,128)(2,1)} %all-reduce.11.cloned.1.call-done), kind=kOutput, calls=%fused_computation.6 | convolution fusion | flops 3760291840 | bytes 19103744 | tf_op jit(solution)/shard_map/dot_general | solution.py:36
  228.6 89.6 %all-reduce.13.cloned.1.call-done = bf16[128,8192]{1,0:T(8,128)(2,1)} async-done(((bf16[128,8192]{1,0:T(8,128)(2,1)}), bf16[128,8192]{1,0:T(8,128)(2,1)}) %all-reduce.13.cloned.1.call-update) | async-done | bytes 2097168 | tf_op jit(solution)/shard_map/psum | solution.py:58
  318.1 5.9 multiply_reduce_fusion
  324.9 26.4 %all-gather.2.cloned.1.call-done = bf16[1024,1024]{1,0:T(8,128)(2,1)} async-done(((bf16[128,1024]{1,0:T(8,128)(2,1)}), bf16[1024,1024]{1,0:T(8,128)(2,1)}) %all-gather.2.cloned.1.call-update) | async-done | bytes 2097168 | tf_op jit(solution)/shard_map/all_gather | solution.py:24
  351.3 3.9 multiply_convert_fusion.3
  355.2 2.6 multiply_convert_fusion.2
  358.6 8.0 %all-reduce.2 = (f32[]{:T(128)}, f32[]{:T(128)}) all-reduce(f32[]{:T(128)} %multiply_reduce_fusion.1, f32[]{:T(128)} %get-tuple-element.18), channel_id=1, replica_groups=mesh['dp_0'=4,'dp_1'=2,'mp_0'=4,'mp_1'=4] {'dp_0'}, use_global_device_ids=true, to_apply=%region_1.0 | all-reduce | flops 2 | bytes 16 | tf_op jit(solution)/shard_map/psum | solution.py:19
  366.6 5.0 all-reduce.3
  371.6 9.9 %all-reduce.1 = (f32[]{:T(128)}, f32[]{:T(128)}) all-reduce(f32[]{:T(128)} %get-tuple-element.8, f32[]{:T(128)} %get-tuple-element.9), channel_id=1, replica_groups=mesh['dp_0'=4,'dp_1'=2,'mp_0'=4,'mp_1'=4] {'mp_0'}, use_global_device_ids=true, to_apply=%region_3.0 | all-reduce | flops 2 | bytes 16 | tf_op jit(solution)/shard_map/psum | solution.py:19
  381.6 9.3 %all-reduce = (f32[]{:T(128)}, f32[]{:T(128)}) all-reduce(f32[]{:T(128)} %get-tuple-element.4, f32[]{:T(128)} %get-tuple-element.5), channel_id=1, replica_groups=mesh['dp_0'=4,'dp_1'=2,'mp_0'=4,'mp_1'=4] {'mp_1'}, use_global_device_ids=true, to_apply=%region_4.0 | all-reduce | flops 2 | bytes 16 | tf_op jit(solution)/shard_map/psum | solution.py:19
  392.1 2.6 fusion.7
  394.7 66.6 %all-reduce.17.cloned.1.call-done = (bf16[8,128,1024]{2,1,0:T(8,128)(2,1)}, bf16[8,128,1024]{2,1,0:T(8,128)(2,1)}) async-done(((bf16[8,128,1024]{2,1,0:T(8,128)(2,1)}, bf16[8,128,1024]{2,1,0:T(8,128)(2,1)}), (bf16[8,128,1024]{2,1,0:T(8,128)(2,1)}, bf16[8,128,1024]{2,1,0:T(8,128)(2,1)})) %all-reduce.17.cloned.1.call-update) | async-done | bytes 4194320 | tf_op jit(solution)/shard_map/psum | solution.py:81
  461.3 9.8 %fusion.10 = f32[8,512,1024]{2,1,0:T(8,128)} fusion(bf16[8,128,512]{2,1,0:T(8,128)(2,1)S(1)} %bitcast.28, bf16[8,128,1024]{2,1,0:T(8,128)(2,1)} %get-tuple-element.12), kind=kOutput, calls=%fused_computation.28 | convolution fusion | flops 1073741824 | bytes 19922944 | tf_op jit(solution)/shard_map/ntr,ntc->nrc/dot_general | solution.py:96
  471.2 11.4 %subtract_convert_fusion.1 = bf16[8,512,1024]{2,1,0:T(8,128)(2,1)} fusion(f32[8,512,1024]{2,1,0:T(8,128)} %fusion.10, bf16[8,128,512]{2,1,0:T(8,128)(2,1)S(1)} %bitcast.30, bf16[8,128,1024]{2,1,0:T(8,128)(2,1)S(1)} %copy-done.4), kind=kOutput, calls=%fused_computation.3 | convolution fusion | flops 1082130432 | bytes 28311552 | tf_op jit(solution)/shard_map/ntr,ntc->nrc/dot_general | solution.py:98
  482.6 5.7 convert_reduce_fusion.1
  490.1 2.6 multiply_convert_fusion
  495.4 103.4 %all-reduce.15.cloned.1.call-done = (bf16[8,128,1024]{2,1,0:T(8,128)(2,1)}, bf16[8,128,1024]{2,1,0:T(8,128)(2,1)}) async-done(((bf16[8,128,1024]{2,1,0:T(8,128)(2,1)}, bf16[8,128,1024]{2,1,0:T(8,128)(2,1)}), (bf16[8,128,1024]{2,1,0:T(8,128)(2,1)}, bf16[8,128,1024]{2,1,0:T(8,128)(2,1)})) %all-reduce.15.cloned.1.call-update) | async-done | bytes 4194320 | tf_op jit(solution)/shard_map/psum | solution.py:81
  598.8 9.8 %fusion.11 = f32[8,512,1024]{2,1,0:T(8,128)} fusion(bf16[8,128,512]{2,1,0:T(8,128)(2,1)S(1)} %bitcast.29, bf16[8,128,1024]{2,1,0:T(8,128)(2,1)} %get-tuple-element.10), kind=kOutput, calls=%fused_computation.29 | convolution fusion | flops 1073741824 | bytes 19922944 | tf_op jit(solution)/shard_map/ntr,ntc->nrc/dot_general | solution.py:96
  608.6 11.7 %subtract_convert_fusion = bf16[8,512,1024]{2,1,0:T(8,128)(2,1)} fusion(f32[8,512,1024]{2,1,0:T(8,128)} %fusion.11, bf16[8,128,512]{2,1,0:T(8,128)(2,1)S(1)} %bitcast.31, bf16[8,128,1024]{2,1,0:T(8,128)(2,1)S(1)} %copy-done.5), kind=kOutput, calls=%fused_computation.1 | convolution fusion | flops 1082130432 | bytes 28311552 | tf_op jit(solution)/shard_map/ntr,ntc->nrc/dot_general | solution.py:98
  620.3 5.7 convert_reduce_fusion
  (37 shorter events, 11.0 us)
Async XLA Ops:
  7.2 201.1 %all-reduce.11.cloned.1.call-start = ((), (), s32[]{:S(2)}) async-start(), calls=%async_computation.1 | async-start | bytes 4194304 | tf_op jit(solution)/shard_map/psum | solution.py:47
  10.2 104.9 %copy-start.8 = (bf16[128,512]{1,0:T(8,128)(2,1)S(1)}, bf16[128,512]{1,0:T(8,128)(2,1)}, u32[]{:S(2)}) copy-start(bf16[128,512]{1,0:T(8,128)(2,1)} %param.4) | copy-start | bytes 393220
  111.9 3.2 copy-start
  119.3 89.0 %copy-start.9 = (bf16[128,896]{1,0:T(8,128)(2,1)S(1)}, bf16[128,896]{1,0:T(8,128)(2,1)}, u32[]{:S(2)}) copy-start(bf16[128,896]{1,0:T(8,128)(2,1)} %param.6) | copy-start | bytes 688132
  119.3 198.8 %all-reduce.13.cloned.1.call-start = ((), (), s32[]{:S(2)}) async-start(), calls=%async_computation.2 | async-start | bytes 4194304 | tf_op jit(solution)/shard_map/psum | solution.py:58
  228.5 122.8 %copy-start.1 = (f32[512,1024]{1,0:T(8,128)S(1)}, f32[512,1024]{1,0:T(8,128)}, u32[]{:S(2)}) copy-start(f32[512,1024]{1,0:T(8,128)} %param.7) | copy-start | bytes 6291460
  228.5 122.8 %all-gather.2.cloned.1.call-start = ((), (), s32[]{:S(2)}) async-start(), calls=%async_computation.3 | async-start | bytes 2359296 | tf_op jit(solution)/shard_map/all_gather | solution.py:24
  324.8 136.5 %all-reduce.17.cloned.1.call-start = ((), (), s32[]{:S(2)}) async-start(), calls=%async_computation.5 | async-start | bytes 8388608 | tf_op jit(solution)/shard_map/psum | solution.py:81
  351.3 4.0 copy-start.6
  357.8 240.9 %all-reduce.15.cloned.1.call-start = ((), (), s32[]{:S(2)}) async-start(), calls=%async_computation.4 | async-start | bytes 8388608 | tf_op jit(solution)/shard_map/psum | solution.py:81
  461.3 9.8 %copy-start.2 = (bf16[1024,512]{1,0:T(8,128)(2,1)S(1)}, bf16[1024,512]{1,0:T(8,128)(2,1)}, u32[]{:S(2)}) copy-start(bf16[1024,512]{1,0:T(8,128)(2,1)} %get-tuple-element.16) | copy-start | bytes 3145732
  461.3 9.8 %copy-start.4 = (bf16[8,128,1024]{2,1,0:T(8,128)(2,1)S(1)}, bf16[8,128,1024]{2,1,0:T(8,128)(2,1)}, u32[]{:S(2)}) copy-start(bf16[8,128,1024]{2,1,0:T(8,128)(2,1)} %get-tuple-element.13) | copy-start | bytes 6291460
  488.3 1.9 copy-start.7
  598.8 9.8 %copy-start.3 = (bf16[1024,512]{1,0:T(8,128)(2,1)S(1)}, bf16[1024,512]{1,0:T(8,128)(2,1)}, u32[]{:S(2)}) copy-start(bf16[1024,512]{1,0:T(8,128)(2,1)} %get-tuple-element.16) | copy-start | bytes 3145732
  598.8 9.8 %copy-start.5 = (bf16[8,128,1024]{2,1,0:T(8,128)(2,1)S(1)}, bf16[8,128,1024]{2,1,0:T(8,128)(2,1)}, u32[]{:S(2)}) copy-start(bf16[8,128,1024]{2,1,0:T(8,128)(2,1)} %get-tuple-element.11) | copy-start | bytes 6291460
Sparse Core Ops, SparseCore 0:
  119.4 88.7 all-reduce.10
  228.6 89.4 all-reduce.12
  324.9 26.2 all-gather.1
  358.0 103.3 all-reduce.16
  495.5 103.2 all-reduce.14
